TPU v7x, 32 devices: a whole 2x2x4 slice. The times are simulated.
32 devices in a mesh: rep: 4 (over y, x), shard: 8 (over z, core).
Axes of the slice: x: 2, y: 2, z: 4, core: 2. Of those that a mesh axis runs over, the one named last changes fastest.
Arguments:
- inputs: bfloat16 [4, 1792, 768], P('rep', 'shard'), may hold values from -6 to 6
- cotangent: bfloat16 [4, 1792, 768], P('rep', 'shard'), may hold values from -6 to 6
- lengths: int32 [4], P('rep'), may hold values from 448 to 1792, as said below
- w_query: bfloat16 [768, 768], P('shard'), may hold values from -0.3125 to 0.3125
- w_key: bfloat16 [768, 768], P('shard'), may hold values from -0.3125 to 0.3125
- w_value: bfloat16 [768, 768], P('shard'), may hold values from -0.21875 to 0.21875
- w_out: bfloat16 [768, 768], P('shard'), may hold values from -1.25 to 1.25
- b_query: bfloat16 [768], P('shard'), may hold values from -1.5 to 1.5
- b_value: bfloat16 [768], P('shard'), may hold values from -0.25 to 0.25
- b_out: bfloat16 [768], P('shard'), may hold values from -1.5 to 1.5
- gain_one: bfloat16 [768], P('shard'), may hold values from 0.5 to 1.5
- shift_one: bfloat16 [768], P('shard'), may hold values from -1.5 to 1.5
- w_up: bfloat16 [768, 3072], P('shard'), may hold values from -0.21875 to 0.21875
- b_up: bfloat16 [3072], P('shard'), may hold values from -1.5 to 1.5
- w_down: bfloat16 [3072, 768], P('shard'), may hold values from -0.15625 to 0.15625
- b_down: bfloat16 [768], P('shard'), may hold values from -1.5 to 1.5
- gain_two: bfloat16 [768], P('shard'), may hold values from 0.5 to 1.5
- shift_two: bfloat16 [768], P('shard'), may hold values from -1.5 to 1.5
Outputs:
- layer_output: bfloat16 [4, 1792, 768], P('rep', 'shard')
- input_grad: float32 [4, 1792, 768], P('rep', 'shard')
- grad_w_query: float32 [768, 768], P('shard')
- grad_w_key: float32 [768, 768], P('shard')
- grad_w_value: float32 [768, 768], P('shard')
- grad_w_out: float32 [768, 768], P('shard')
- grad_b_query: float32 [768], P('shard')
- grad_b_value: float32 [768], P('shard')
- grad_b_out: float32 [768], P('shard')
- grad_gain_one: float32 [768], P('shard')
- grad_shift_one: float32 [768], P('shard')
- grad_w_up: float32 [768, 3072], P('shard')
- grad_b_up: float32 [3072], P('shard')
- grad_w_down: float32 [3072, 768], P('shard')
- grad_b_down: float32 [768], P('shard')
- grad_gain_two: float32 [768], P('shard')
- grad_shift_two: float32 [768], P('shard')
Inputs may be any that keep to these rules, and one draw needn't show every extreme that they name: `lengths`: slot 0 is full; the others hold between a quarter of 1792 and 1792 valid tokens.
All inputs are finite; a program needn't handle non-finite values.
Results may differ from a plain program's by a relative error of at most 0.024.
Values may be sent and summed in bfloat16 or wider, within the bound.
No kernel may reach another device: no remote copies, remote signals or barrier semaphores. Data moves between devices by JAX's collectives and lax.ppermute only.
A program may use at most 256 MiB of HBM per device.

v0:
```python
import math
import jax
import jax.numpy as jnp
from jax import lax
from jax.sharding import PartitionSpec as P

HEADS = 12
HEAD_DIM = 64
epsilon = 1e-05
floor_value = -1e30


def inner_rows(left, right):
    return lax.dot_general(
        left, right, (((0,), (0,)), ((), ())), preferred_element_type=jnp.float32
    )


def times_transposed(left, right):
    return lax.dot_general(
        left, right, (((1,), (1,)), ((), ())), preferred_element_type=jnp.float32
    )


def plain_product(left, right):
    return jnp.dot(left, right, preferred_element_type=jnp.float32)


def norm_forward(hidden, gain, shift):
    center = hidden - jnp.mean(hidden, axis=1, keepdims=True)
    inverse = lax.rsqrt(jnp.mean(center * center, axis=1, keepdims=True) + epsilon)
    scaled = center * inverse
    return (scaled * gain.astype(jnp.float32) + shift.astype(jnp.float32), scaled, inverse)


def norm_backward(grad_out, gain, scaled, inverse):
    grad_scaled = grad_out * gain.astype(jnp.float32)
    grad_in = inverse * (
        grad_scaled
        - jnp.mean(grad_scaled, axis=1, keepdims=True)
        - scaled * jnp.mean(grad_scaled * scaled, axis=1, keepdims=True)
    )
    return (grad_in, jnp.sum(grad_out * scaled, axis=0), jnp.sum(grad_out, axis=0))


def gelu_both(upward):
    cumulative = 0.5 * (1.0 + lax.erf(upward * 0.7071067811865476))
    density = jnp.exp(-0.5 * upward * upward) * 0.3989422804014327
    return (upward * cumulative, cumulative + upward * density)


def split_heads(rows):
    return rows.reshape(rows.shape[0], HEADS, HEAD_DIM)


def column_sum(values_low):
    return jnp.sum(values_low.astype(jnp.float32), axis=0)


def body(
    inputs,
    cotangent,
    lengths,
    w_query,
    w_key,
    w_value,
    w_out,
    b_query,
    b_value,
    b_out,
    gain_one,
    shift_one,
    w_up,
    b_up,
    w_down,
    b_down,
    gain_two,
    shift_two,
):
    gathered = (
        lax.all_gather(w_query, "shard", axis=0, tiled=True),
        lax.all_gather(w_key, "shard", axis=0, tiled=True),
        lax.all_gather(w_value, "shard", axis=0, tiled=True),
        lax.all_gather(w_out, "shard", axis=0, tiled=True),
        lax.all_gather(b_query, "shard", axis=0, tiled=True),
        lax.all_gather(b_value, "shard", axis=0, tiled=True),
        lax.all_gather(b_out, "shard", axis=0, tiled=True),
        lax.all_gather(gain_one, "shard", axis=0, tiled=True),
        lax.all_gather(shift_one, "shard", axis=0, tiled=True),
        lax.all_gather(w_up, "shard", axis=0, tiled=True),
        lax.all_gather(b_up, "shard", axis=0, tiled=True),
        lax.all_gather(w_down, "shard", axis=0, tiled=True),
        lax.all_gather(b_down, "shard", axis=0, tiled=True),
        lax.all_gather(gain_two, "shard", axis=0, tiled=True),
        lax.all_gather(shift_two, "shard", axis=0, tiled=True),
    )
    (
        query_full,
        key_full,
        value_full,
        out_full,
        bias_query,
        bias_value,
        bias_out,
        gain_first,
        shift_first,
        up_full,
        bias_up,
        down_full,
        bias_down,
        gain_second,
        shift_second,
    ) = gathered
    tokens = inputs[0]
    rows = tokens.shape[0]
    model = tokens.shape[1]
    scale = HEAD_DIM ** (-0.5)
    length = lengths[0]
    positions = lax.axis_index("shard") * rows + jnp.arange(rows, dtype=jnp.int32)
    own_valid = positions < length
    row_valid = own_valid.astype(jnp.float32)
    source = tokens.astype(jnp.float32)
    query = (plain_product(tokens, query_full) + bias_query.astype(jnp.float32)).astype(
        jnp.bfloat16
    )
    keys = plain_product(tokens, key_full).astype(jnp.bfloat16)
    values = (plain_product(tokens, value_full) + bias_value.astype(jnp.float32)).astype(
        jnp.bfloat16
    )
    pairs = lax.all_gather(jnp.concatenate([keys, values], axis=1), "shard", axis=0, tiled=True)
    total = pairs.shape[0]
    block = math.gcd(total, 1024)
    count = total // block
    query_heads = split_heads(query)

    def block_scores(index):
        start = index * block
        piece = lax.dynamic_slice_in_dim(pairs, start, block, 0)
        key_heads = split_heads(piece[:, :model])
        value_heads = split_heads(piece[:, model:])
        scores = (
            jnp.einsum("qhd,khd->hqk", query_heads, key_heads, preferred_element_type=jnp.float32)
            * scale
        )
        key_valid = start + jnp.arange(block, dtype=jnp.int32) < length
        return (scores, key_valid[None, None, :], key_heads, value_heads)

    def running_max(index, carry):
        highest, summed = carry
        scores, key_valid, key_heads, value_heads = block_scores(index)
        masked = jnp.where(key_valid, scores, floor_value)
        newest = jnp.maximum(highest, jnp.max(masked, axis=2))
        weights = jnp.where(key_valid, jnp.exp(masked - newest[:, :, None]), 0.0)
        return (newest, summed * jnp.exp(highest - newest) + jnp.sum(weights, axis=2))

    start_max = jnp.full((HEADS, rows), floor_value, jnp.float32)
    highest, summed = lax.fori_loop(
        0, count, running_max, (start_max, jnp.zeros((HEADS, rows), jnp.float32))
    )
    log_total = highest + jnp.log(summed)

    def weighted(index, mixed_sum):
        scores, key_valid, key_heads, value_heads = block_scores(index)
        probs = jnp.where(key_valid, jnp.exp(scores - log_total[:, :, None]), 0.0).astype(
            jnp.bfloat16
        )
        return mixed_sum + jnp.einsum(
            "hqk,khd->qhd", probs, value_heads, preferred_element_type=jnp.float32
        )

    mixed = lax.fori_loop(0, count, weighted, jnp.zeros((rows, HEADS, HEAD_DIM), jnp.float32))
    mixed_low = mixed.reshape(rows, model).astype(jnp.bfloat16)
    branch = plain_product(mixed_low, out_full) + bias_out.astype(jnp.float32)
    normed, scaled_one, inverse_one = norm_forward(source + branch, gain_first, shift_first)
    normed_low = normed.astype(jnp.bfloat16)
    upward = plain_product(normed_low, up_full) + bias_up.astype(jnp.float32)
    active, slope = gelu_both(upward)
    active_low = active.astype(jnp.bfloat16)
    second = plain_product(active_low, down_full) + bias_down.astype(jnp.float32)
    result, scaled_two, inverse_two = norm_forward(normed + second, gain_second, shift_second)
    backward_params = (
        lax.all_gather(w_query, "shard", axis=0, tiled=True),
        lax.all_gather(w_key, "shard", axis=0, tiled=True),
        lax.all_gather(w_value, "shard", axis=0, tiled=True),
        lax.all_gather(w_out, "shard", axis=0, tiled=True),
        lax.all_gather(b_query, "shard", axis=0, tiled=True),
        lax.all_gather(b_value, "shard", axis=0, tiled=True),
        lax.all_gather(b_out, "shard", axis=0, tiled=True),
        lax.all_gather(gain_one, "shard", axis=0, tiled=True),
        lax.all_gather(shift_one, "shard", axis=0, tiled=True),
        lax.all_gather(w_up, "shard", axis=0, tiled=True),
        lax.all_gather(b_up, "shard", axis=0, tiled=True),
        lax.all_gather(w_down, "shard", axis=0, tiled=True),
        lax.all_gather(b_down, "shard", axis=0, tiled=True),
        lax.all_gather(gain_two, "shard", axis=0, tiled=True),
        lax.all_gather(shift_two, "shard", axis=0, tiled=True),
    )
    query_back = backward_params[0]
    key_back = backward_params[1]
    value_back = backward_params[2]
    out_back = backward_params[3]
    gain_first_back = backward_params[7]
    up_back = backward_params[9]
    down_back = backward_params[11]
    gain_second_back = backward_params[13]
    grad_result = cotangent[0].astype(jnp.float32) * row_valid[:, None]
    grad_sum_two, grad_gain_second, grad_shift_second = norm_backward(
        grad_result, gain_second_back, scaled_two, inverse_two
    )
    grad_second = grad_sum_two.astype(jnp.bfloat16)
    grad_down = inner_rows(active_low, grad_second)
    grad_bias_down = column_sum(grad_second)
    grad_upward = (times_transposed(grad_second, down_back) * slope).astype(jnp.bfloat16)
    grad_up = inner_rows(normed_low, grad_upward)
    grad_bias_up = column_sum(grad_upward)
    grad_normed = grad_sum_two + times_transposed(grad_upward, up_back)
    grad_sum_one, grad_gain_first, grad_shift_first = norm_backward(
        grad_normed, gain_first_back, scaled_one, inverse_one
    )
    grad_branch = grad_sum_one.astype(jnp.bfloat16)
    grad_out_proj = inner_rows(mixed_low, grad_branch)
    grad_bias_out = column_sum(grad_branch)
    grad_mixed = times_transposed(grad_branch, out_back).astype(jnp.bfloat16)
    grad_mixed_heads = split_heads(grad_mixed)
    delta = jnp.einsum("qhd,qhd->hq", grad_mixed_heads.astype(jnp.float32), mixed)

    def key_grads(index, carry):
        grad_query_sum, buffer = carry
        scores, key_valid, key_heads, value_heads = block_scores(index)
        probs = jnp.where(key_valid, jnp.exp(scores - log_total[:, :, None]), 0.0)
        probs_low = probs.astype(jnp.bfloat16)
        grad_probs = jnp.einsum(
            "qhd,khd->hqk", grad_mixed_heads, value_heads, preferred_element_type=jnp.float32
        )
        grad_scores = (probs * (grad_probs - delta[:, :, None])).astype(jnp.bfloat16)
        grad_query_sum = (
            grad_query_sum
            + jnp.einsum("hqk,khd->qhd", grad_scores, key_heads, preferred_element_type=jnp.float32)
            * scale
        )
        key_part = (
            jnp.einsum("hqk,qhd->khd", grad_scores, query_heads, preferred_element_type=jnp.float32)
            * scale
        )
        value_part = jnp.einsum(
            "hqk,qhd->khd", probs_low, grad_mixed_heads, preferred_element_type=jnp.float32
        )
        update = jnp.concatenate(
            [key_part.reshape(block, model), value_part.reshape(block, model)], axis=1
        )
        buffer = lax.dynamic_update_slice_in_dim(buffer, update, index * block, 0)
        return (grad_query_sum, buffer)

    grad_query_sum, buffer = lax.fori_loop(
        0,
        count,
        key_grads,
        (
            jnp.zeros((rows, HEADS, HEAD_DIM), jnp.float32),
            jnp.zeros((total, 2 * model), jnp.float32),
        ),
    )
    grad_pairs = lax.psum_scatter(
        buffer.astype(jnp.bfloat16), "shard", scatter_dimension=0, tiled=True
    ).astype(jnp.float32)
    grad_query = grad_query_sum.reshape(rows, model)
    grad_keys = grad_pairs[:, :model]
    grad_values = grad_pairs[:, model:]
    query_low = grad_query.astype(jnp.bfloat16)
    keys_low = grad_keys.astype(jnp.bfloat16)
    values_low = grad_values.astype(jnp.bfloat16)
    grad_query_proj = inner_rows(tokens, query_low)
    grad_key_proj = inner_rows(tokens, keys_low)
    grad_value_proj = inner_rows(tokens, values_low)
    grad_bias_query = column_sum(query_low)
    grad_bias_value = column_sum(values_low)
    grad_input = (
        grad_sum_one
        + times_transposed(query_low, query_back)
        + times_transposed(keys_low, key_back)
        + times_transposed(values_low, value_back)
    )
    shared = (
        lax.psum_scatter(
            grad_query_proj.astype(jnp.bfloat16), "shard", scatter_dimension=0, tiled=True
        ).astype(jnp.float32),
        lax.psum_scatter(
            grad_key_proj.astype(jnp.bfloat16), "shard", scatter_dimension=0, tiled=True
        ).astype(jnp.float32),
        lax.psum_scatter(
            grad_value_proj.astype(jnp.bfloat16), "shard", scatter_dimension=0, tiled=True
        ).astype(jnp.float32),
        lax.psum_scatter(
            grad_out_proj.astype(jnp.bfloat16), "shard", scatter_dimension=0, tiled=True
        ).astype(jnp.float32),
        lax.psum_scatter(
            grad_bias_query.astype(jnp.bfloat16), "shard", scatter_dimension=0, tiled=True
        ).astype(jnp.float32),
        lax.psum_scatter(
            grad_bias_value.astype(jnp.bfloat16), "shard", scatter_dimension=0, tiled=True
        ).astype(jnp.float32),
        lax.psum_scatter(
            grad_bias_out.astype(jnp.bfloat16), "shard", scatter_dimension=0, tiled=True
        ).astype(jnp.float32),
        lax.psum_scatter(
            grad_gain_first.astype(jnp.bfloat16), "shard", scatter_dimension=0, tiled=True
        ).astype(jnp.float32),
        lax.psum_scatter(
            grad_shift_first.astype(jnp.bfloat16), "shard", scatter_dimension=0, tiled=True
        ).astype(jnp.float32),
        lax.psum_scatter(
            grad_up.astype(jnp.bfloat16), "shard", scatter_dimension=0, tiled=True
        ).astype(jnp.float32),
        lax.psum_scatter(
            grad_bias_up.astype(jnp.bfloat16), "shard", scatter_dimension=0, tiled=True
        ).astype(jnp.float32),
        lax.psum_scatter(
            grad_down.astype(jnp.bfloat16), "shard", scatter_dimension=0, tiled=True
        ).astype(jnp.float32),
        lax.psum_scatter(
            grad_bias_down.astype(jnp.bfloat16), "shard", scatter_dimension=0, tiled=True
        ).astype(jnp.float32),
        lax.psum_scatter(
            grad_gain_second.astype(jnp.bfloat16), "shard", scatter_dimension=0, tiled=True
        ).astype(jnp.float32),
        lax.psum_scatter(
            grad_shift_second.astype(jnp.bfloat16), "shard", scatter_dimension=0, tiled=True
        ).astype(jnp.float32),
    )
    (
        part_query,
        part_key,
        part_value,
        part_out,
        part_bias_query,
        part_bias_value,
        part_bias_out,
        part_gain_first,
        part_shift_first,
        part_up,
        part_bias_up,
        part_down,
        part_bias_down,
        part_gain_second,
        part_shift_second,
    ) = shared
    summed = (
        lax.psum(part_query.astype(jnp.bfloat16), "rep").astype(jnp.float32),
        lax.psum(part_key.astype(jnp.bfloat16), "rep").astype(jnp.float32),
        lax.psum(part_value.astype(jnp.bfloat16), "rep").astype(jnp.float32),
        lax.psum(part_out.astype(jnp.bfloat16), "rep").astype(jnp.float32),
        lax.psum(part_bias_query.astype(jnp.bfloat16), "rep").astype(jnp.float32),
        lax.psum(part_bias_value.astype(jnp.bfloat16), "rep").astype(jnp.float32),
        lax.psum(part_bias_out.astype(jnp.bfloat16), "rep").astype(jnp.float32),
        lax.psum(part_gain_first.astype(jnp.bfloat16), "rep").astype(jnp.float32),
        lax.psum(part_shift_first.astype(jnp.bfloat16), "rep").astype(jnp.float32),
        lax.psum(part_up.astype(jnp.bfloat16), "rep").astype(jnp.float32),
        lax.psum(part_bias_up.astype(jnp.bfloat16), "rep").astype(jnp.float32),
        lax.psum(part_down.astype(jnp.bfloat16), "rep").astype(jnp.float32),
        lax.psum(part_bias_down.astype(jnp.bfloat16), "rep").astype(jnp.float32),
        lax.psum(part_gain_second.astype(jnp.bfloat16), "rep").astype(jnp.float32),
        lax.psum(part_shift_second.astype(jnp.bfloat16), "rep").astype(jnp.float32),
    )
    return (result.astype(jnp.bfloat16)[None], grad_input[None]) + tuple(summed)


def solution(mesh):
    placed = (
        P("rep", "shard", None),
        P("rep", "shard", None),
        P("rep"),
        P("shard", None),
        P("shard", None),
        P("shard", None),
        P("shard", None),
        P("shard"),
        P("shard"),
        P("shard"),
        P("shard"),
        P("shard"),
        P("shard", None),
        P("shard"),
        P("shard", None),
        P("shard"),
        P("shard"),
        P("shard"),
    )
    return jax.shard_map(
        body,
        mesh=mesh,
        in_specs=placed,
        out_specs=(
            P("rep", "shard", None),
            P("rep", "shard", None),
            P("shard", None),
            P("shard", None),
            P("shard", None),
            P("shard", None),
            P("shard"),
            P("shard"),
            P("shard"),
            P("shard"),
            P("shard"),
            P("shard", None),
            P("shard"),
            P("shard", None),
            P("shard"),
            P("shard"),
            P("shard"),
        ),
        check_vma=False,
    )
```

profile of v0, /device:TPU:0, one launch (start us, length us, event | category | flops | bytes accessed | tf_op | source)
XLA Modules:
  0.0 737.3 jit_solution(4788529265016331617)
XLA Ops:
  17.3 30.8 %all-reduce.18 = (bf16[768]{0:T(1024)(128)(2,1)S(1)}, bf16[768]{0:T(1024)(128)(2,1)S(1)}, bf16[768]{0:T(1024)(128)(2,1)S(1)}, bf16[768]{0:T(1024)(128)(2,1)S(1)}...) all-reduce(bf16[768]{0:T(1024)(128)(2,1)S(1)} %dynamic-update-slice, ...), channel_id=1, replica_groups=mesh['rep'=4,'shard'=8] {'shard'}, use_global_device_ids=true, to_apply=%add | all-reduce | flops 5376 | bytes 21504
  50.0 9.5 %all-gather.11.cloned.1.call-done = bf16[768,768]{1,0:T(8,128)(2,1)} async-done(((bf16[96,768]{1,0:T(8,128)(2,1)}), bf16[768,768]{1,0:T(8,128)(2,1)}) %all-gather.11.cloned.1.call-update) | async-done | bytes 1179664 | tf_op jit(solution)/shard_map/all_gather | solution.py:83
  64.9 13.0 %all-gather = bf16[8,1,384]{2,1,0:T(2,128)(2,1)S(1)} all-gather(bf16[1,1,384]{2,1,0:T(2,128)(2,1)S(1)} %reshape.198), channel_id=1, replica_groups=mesh['rep'=4,'shard'=8] {'shard'}, dimensions={0}, use_global_device_ids=true | all-gather | bytes 6912 | tf_op jit(solution)/shard_map/all_gather | solution.py:91
  78.0 5.5 all-gather.15.cloned.1.call-done
  85.4 58.1 %all-gather.13.cloned.1.call-done = bf16[1792,1536]{1,0:T(8,128)(2,1)} async-done(((bf16[224,1536]{1,0:T(8,128)(2,1)}), bf16[1792,1536]{1,0:T(8,128)(2,1)}) %all-gather.13.cloned.1.call-update) | async-done | bytes 5505040 | tf_op jit(solution)/shard_map/all_gather | solution.py:130
  143.5 8.3 %copy.55 = bf16[1792,1536]{0,1:T(8,128)(2,1)} copy(bf16[1792,1536]{1,0:T(8,128)(2,1)} %all-gather.13.cloned.1.call-done) | data formatting | bytes 11010048
  151.8 25.8 %while.46 = (s32[]{:T(128)}, f32[12,224]{1,0:T(8,128)S(1)}, f32[12,224]{1,0:T(8,128)S(1)}, s32[]{:T(128)}, bf16[1792,1536]{0,1:T(8,128)(2,1)}, /*index=5*/bf16[2...) while((s32[]{:T(128)}, f32[12,224]{1,0:T(8,128)S(1)}, ...), condition=%wide.region_3.4_spmd.clone, body=%wide.region_0.3_spmd.clone.sunk | while | flops 93599368 | bytes 7169458 | solution.py:157
  177.6 34.2 %while.47 = (s32[]{:T(128)}, f32[224,12,64]{0,2,1:T(8,128)}, bf16[1792,1536]{0,1:T(8,128)(2,1)}, s32[]{:T(128)}, bf16[224,12,64]{0,2,1:T(8,128)(2,1)S(1)}, /*ind...) while((s32[]{:T(128)}, f32[224,12,64]{0,2,1:T(8,128)}, ...), condition=%wide.region_5.6_spmd.clone, body=%wide.region_4.5_spmd.clone.sunk | while | flops 179257856 | bytes 4091081 | solution.py:171
  218.9 5.9 multiply_convert_fusion.1
  224.8 45.7 %all-gather.21.cloned.1.call-done = bf16[3072,768]{1,0:T(8,128)(2,1)} async-done(((bf16[384,768]{1,0:T(8,128)(2,1)}), bf16[3072,768]{1,0:T(8,128)(2,1)}) %all-gather.21.cloned.1.call-update) | async-done | bytes 4718608 | tf_op jit(solution)/shard_map/all_gather | solution.py:92
  290.3 44.6 %while.48 = (s32[]{:T(128)}, f32[224,12,64]{0,2,1:T(8,128)S(1)}, bf16[1792,1536]{0,1:T(8,128)(2,1)}, bf16[1792,1536]{0,1:T(8,128)(2,1)}, s32[]{:T(128)}, /*index...) while((s32[]{:T(128)}, f32[224,12,64]{0,2,1:T(8,128)S(1)}, ...), condition=%wide.region_15.16_spmd.clone, body=%wide.region_14.15_spmd.clone.sunk | while | flops 449765888 | bytes 21660160 | solution.py:254
  334.8 8.3 %copy.69 = bf16[1792,1536]{1,0:T(8,128)(2,1)} copy(bf16[1792,1536]{0,1:T(8,128)(2,1)} %get-tuple-element.395) | data formatting | bytes 11010048
  348.1 56.3 %reduce-scatter.22.cloned.1.call-done = bf16[224,1536]{1,0:T(8,128)(2,1)} async-done(((bf16[1792,1536]{1,0:T(8,128)(2,1)}), bf16[224,1536]{1,0:T(8,128)(2,1)}) %reduce-scatter.22.cloned.1.call-update) | async-done | bytes 688144
  416.0 5.0 convolution_convert_fusion.1
  422.4 4.7 convolution_convert_fusion
  427.2 11.5 %reduce-scatter.24.cloned.1.call-done = bf16[96,768]{1,0:T(8,128)(2,1)} async-done(((bf16[768,768]{1,0:T(8,128)(2,1)}), bf16[96,768]{1,0:T(8,128)(2,1)}) %reduce-scatter.24.cloned.1.call-update) | async-done | bytes 147472
  440.4 31.5 %reduce-scatter.28.cloned.1.call-done = bf16[96,768]{1,0:T(8,128)(2,1)} async-done(((bf16[768,768]{1,0:T(8,128)(2,1)}), bf16[96,768]{1,0:T(8,128)(2,1)}) %reduce-scatter.28.cloned.1.call-update) | async-done | bytes 147472
  473.7 31.9 %reduce-scatter.26.cloned.1.call-done = bf16[96,768]{1,0:T(8,128)(2,1)} async-done(((bf16[768,768]{1,0:T(8,128)(2,1)}), bf16[96,768]{1,0:T(8,128)(2,1)}) %reduce-scatter.26.cloned.1.call-update) | async-done | bytes 147472
  507.3 32.0 %reduce-scatter.16.cloned.1.call-done = bf16[96,768]{1,0:T(8,128)(2,1)} async-done(((bf16[768,768]{1,0:T(8,128)(2,1)}), bf16[96,768]{1,0:T(8,128)(2,1)}) %reduce-scatter.16.cloned.1.call-update) | async-done | bytes 147472 | tf_op jit(solution)/shard_map/reduce_scatter | solution.py:293
  539.3 55.5 %reduce-scatter.18.cloned.1.call-done = bf16[96,3072]{1,0:T(8,128)(2,1)} async-done(((bf16[768,3072]{1,0:T(8,128)(2,1)}), bf16[96,3072]{1,0:T(8,128)(2,1)}) %reduce-scatter.18.cloned.1.call-update) | async-done | bytes 589840 | tf_op jit(solution)/shard_map/reduce_scatter | solution.py:311
  594.8 55.5 %reduce-scatter.20.cloned.1.call-done = bf16[384,768]{1,0:T(8,128)(2,1)} async-done(((bf16[3072,768]{1,0:T(8,128)(2,1)}), bf16[384,768]{1,0:T(8,128)(2,1)}) %reduce-scatter.20.cloned.1.call-update) | async-done | bytes 589840 | tf_op jit(solution)/shard_map/reduce_scatter | solution.py:317
  654.9 26.0 %all-reduce.17 = (bf16[768]{0:T(1024)(128)(2,1)S(1)}, bf16[768]{0:T(1024)(128)(2,1)S(1)}, bf16[768]{0:T(1024)(128)(2,1)S(1)}, bf16[768]{0:T(1024)(128)(2,1)S(1)}...) all-reduce(bf16[768]{0:T(1024)(128)(2,1)S(1)} %dynamic-update-slice, ...), channel_id=1, replica_groups=mesh['rep'=4,'shard'=8] {'shard'}, use_global_device_ids=true, to_apply=%add.7 | all-reduce | flops 9984 | bytes 39936
  681.6 10.0 %all-reduce.19 = (bf16[96]{0:T(256)(128)(2,1)S(1)}, bf16[96]{0:T(256)(128)(2,1)S(1)}, bf16[96]{0:T(256)(128)(2,1)S(1)}, bf16[96]{0:T(256)(128)(2,1)S(1)}, bf16[9...) all-reduce(bf16[96]{0:T(256)(128)(2,1)S(1)} %dynamic-slice.9, ...), channel_id=1, replica_groups=mesh['rep'=4,'shard'=8] {'rep'}, use_global_device_ids=true, to_apply=%region_27.28 | all-reduce | flops 1152 | bytes 4608 | tf_op jit(solution)/shard_map/psum | solution.py:352
  700.3 20.3 %all-reduce.23.cloned.1.call-done = (bf16[96,768]{0,1:T(8,128)(2,1)}, bf16[96,768]{0,1:T(8,128)(2,1)}, bf16[96,768]{0,1:T(8,128)(2,1)}, bf16[96,768]{1,0:T(8,128...) async-done(((bf16[96,768]{0,1:T(8,128)(2,1)}, bf16[96,768]{0,1:T(8,128)(2,1)}, bf16[96,768]{0,1:T(8,128)(2,1)}, bf16[96,768]{1,0:T(8,128)(2,1)}, ...) | async-done | bytes 1769488 | tf_op jit(solution)/shard_map/psum | solution.py:348
  (329 shorter events, 194.0 us)
Async XLA Ops:
  7.2 40.9 %all-gather.9.cloned.1.call-start = ((), (), s32[]{:S(2)}) async-start(), calls=%async_computation.7 | async-start | bytes 1327104 | tf_op jit(solution)/shard_map/all_gather | solution.py:82
  7.9 51.5 %all-gather.11.cloned.1.call-start = ((), (), s32[]{:S(2)}) async-start(), calls=%async_computation.8 | async-start | bytes 1327104 | tf_op jit(solution)/shard_map/all_gather | solution.py:83
  8.7 74.8 %all-gather.15.cloned.1.call-start = ((), (), s32[]{:S(2)}) async-start(), calls=%async_computation.10 | async-start | bytes 1327104 | tf_op jit(solution)/shard_map/all_gather | solution.py:81
  9.4 134.1 %all-gather.13.cloned.1.call-start = ((), (), s32[]{:S(2)}) async-start(), calls=%async_computation.9 | async-start | bytes 6193152 | tf_op jit(solution)/shard_map/all_gather | solution.py:130
  62.2 150.9 %all-gather.17.cloned.1.call-start = ((), (), s32[]{:S(2)}) async-start(), calls=%async_computation.11 | async-start | bytes 1327104 | tf_op jit(solution)/shard_map/all_gather | solution.py:84
  62.8 156.2 %all-gather.19.cloned.1.call-start = ((), (), s32[]{:S(2)}) async-start(), calls=%async_computation.12 | async-start | bytes 5308416 | tf_op jit(solution)/shard_map/all_gather | solution.py:90
  63.4 207.2 %all-gather.21.cloned.1.call-start = ((), (), s32[]{:S(2)}) async-start(), calls=%async_computation.13 | async-start | bytes 5308416 | tf_op jit(solution)/shard_map/all_gather | solution.py:92
  64.1 340.3 %reduce-scatter.22.cloned.1.call-start = ((), (), s32[]{:S(2)}) async-start(), calls=%async_computation.17 | async-start | bytes 6193152
  343.2 95.5 %reduce-scatter.24.cloned.1.call-start = ((), (), s32[]{:S(2)}) async-start(), calls=%async_computation.18 | async-start | bytes 1327104
  348.0 123.9 %reduce-scatter.28.cloned.1.call-start = ((), (), s32[]{:S(2)}) async-start(), calls=%async_computation.20 | async-start | bytes 1327104
  409.4 96.2 %reduce-scatter.26.cloned.1.call-start = ((), (), s32[]{:S(2)}) async-start(), calls=%async_computation.19 | async-start | bytes 1327104
  413.4 125.9 %reduce-scatter.16.cloned.1.call-start = ((), (), s32[]{:S(2)}) async-start(), calls=%async_computation.14 | async-start | bytes 1327104 | tf_op jit(solution)/shard_map/reduce_scatter | solution.py:293
  415.9 178.8 %reduce-scatter.18.cloned.1.call-start = ((), (), s32[]{:S(2)}) async-start(), calls=%async_computation.15 | async-start | bytes 5308416 | tf_op jit(solution)/shard_map/reduce_scatter | solution.py:311
  421.1 229.2 %reduce-scatter.20.cloned.1.call-start = ((), (), s32[]{:S(2)}) async-start(), calls=%async_computation.16 | async-start | bytes 5308416 | tf_op jit(solution)/shard_map/reduce_scatter | solution.py:317
  427.1 224.5 %copy-start.22 = (bf16[96]{0:T(256)(128)(2,1)S(1)}, bf16[96]{0:T(256)(128)(2,1)}, u32[]{:S(2)}) copy-start(bf16[96]{0:T(256)(128)(2,1)} %param.41) | copy-start | bytes 580
  427.1 293.4 %all-reduce.23.cloned.1.call-start = ((), (), s32[]{:S(2)}) async-start(), calls=%async_computation.21 | async-start | bytes 3833856 | tf_op jit(solution)/shard_map/psum | solution.py:348
  473.6 181.2 %copy-start.14 = (bf16[768]{0:T(1024)(128)(2,1)S(1)}, bf16[768]{0:T(1024)(128)(2,1)}, u32[]{:S(2)}) copy-start(bf16[768]{0:T(1024)(128)(2,1)} %get-tuple-element.584) | copy-start | bytes 4612
  473.6 181.2 %copy-start.15 = (bf16[768]{0:T(1024)(128)(2,1)S(1)}, bf16[768]{0:T(1024)(128)(2,1)}, u32[]{:S(2)}) copy-start(bf16[768]{0:T(1024)(128)(2,1)} %get-tuple-element.589) | copy-start | bytes 4612
  473.6 181.2 %copy-start.16 = (bf16[768]{0:T(1024)(128)(2,1)S(1)}, bf16[768]{0:T(1024)(128)(2,1)}, u32[]{:S(2)}) copy-start(bf16[768]{0:T(1024)(128)(2,1)} %get-tuple-element.664) | copy-start | bytes 4612
  473.6 181.2 %copy-start.17 = (bf16[768]{0:T(1024)(128)(2,1)S(1)}, bf16[768]{0:T(1024)(128)(2,1)}, u32[]{:S(2)}) copy-start(bf16[768]{0:T(1024)(128)(2,1)} %get-tuple-element.666) | copy-start | bytes 4612
  473.6 181.2 %copy-start.18 = (bf16[3072]{0:T(1024)(128)(2,1)S(1)}, bf16[3072]{0:T(1024)(128)(2,1)}, u32[]{:S(2)}) copy-start(bf16[3072]{0:T(1024)(128)(2,1)} %get-tuple-element.685) | copy-start | bytes 18436
  473.7 181.2 %copy-start.19 = (bf16[768]{0:T(1024)(128)(2,1)S(1)}, bf16[768]{0:T(1024)(128)(2,1)}, u32[]{:S(2)}) copy-start(bf16[768]{0:T(1024)(128)(2,1)} %get-tuple-element.582) | copy-start | bytes 4612
  473.7 181.2 %copy-start.20 = (bf16[768]{0:T(1024)(128)(2,1)S(1)}, bf16[768]{0:T(1024)(128)(2,1)}, u32[]{:S(2)}) copy-start(bf16[768]{0:T(1024)(128)(2,1)} %get-tuple-element.587) | copy-start | bytes 4612
  507.3 189.1 %copy-start.2 = (bf16[768,768]{1,0:T(8,128)(2,1)S(1)}, bf16[768,768]{1,0:T(8,128)(2,1)}, u32[]{:S(2)}) copy-start(bf16[768,768]{1,0:T(8,128)(2,1)} %all-gather.9.cloned.1.call-done) | copy-start | bytes 3538948
  (25 other events, 135.2 us)
Sparse Core Ops, SparseCore 0:
  9.6 25.6 all-gather.8
  36.9 22.4 all-gather.10
  61.1 22.3 all-gather.14
  85.6 57.9 all-gather.12
  145.0 21.5 all-gather.16
  168.1 50.8 all-gather.18
  220.6 49.9 all-gather.20
  343.3 61.0 reduce-scatter.21
  407.2 31.3 reduce-scatter.23
  440.8 31.0 reduce-scatter.27
  474.2 31.2 reduce-scatter.25
  508.2 30.9 reduce-scatter.15
  541.6 53.1 reduce-scatter.17
  596.9 53.3 reduce-scatter.19
  654.6 65.8 all-reduce.22
where the time goes:
time: 740 us; the launch traced here: 737 us
  waiting for transfers between devices  421 us (57%)
  matrix products  97.8 us (13%)
  blocking collectives  79.9 us (11%)
  local copies, waits for them, and re-layouts  73.4 us (10%)
  other arithmetic  46.9 us (6%)
  between operations  17 us (2%)
    unnamed x19, waiting for transfers between devices  135 us
    all_gather x1, waiting for transfers between devices, body(): lax.all_gather(jnp.concatenate([keys, values], axis=1), 'shard', axis=0,...  58.1 us
    unnamed x2, blocking collectives  56.8 us
    reduce_scatter x1, waiting for transfers between devices, body(): lax.psum_scatter(grad_up.astype(jnp.bfloat16), 'shard', scatter_dimension...  55.5 us
    reduce_scatter x1, waiting for transfers between devices, body(): lax.psum_scatter(grad_down.astype(jnp.bfloat16), 'shard', scatter_dimensi...  55.5 us
    all_gather x1, waiting for transfers between devices, body(): lax.all_gather(w_down, 'shard', axis=0, tiled=True)  45.7 us
    unnamed x92, local copies, waits for them, and re-layouts  44.5 us
    reduce_scatter x1, waiting for transfers between devices, body(): lax.psum_scatter(grad_out_proj.astype(jnp.bfloat16), 'shard', scatter_dim...  32 us
  transfers between devices with their start and end apart: 15, of which 13 were waited for; matrix products, arithmetic and copies ran while one was open for 18% of the time, Pallas kernels for 0%

commit v1 on v0

--- a/solution.py
+++ b/solution.py
@@ -8,6 +8,11 @@
 HEAD_DIM = 64
 epsilon = 1e-05
 floor_value = -1e30
+
+
+def summed_here(x, mesh_axis):
+    shards = lax.all_gather(x, mesh_axis)
+    return jnp.sum(shards, axis=0)
 
 
 def inner_rows(left, right):
@@ -345,7 +350,7 @@
         part_shift_second,
     ) = shared
     summed = (
-        lax.psum(part_query.astype(jnp.bfloat16), "rep").astype(jnp.float32),
+        summed_here(part_query.astype(jnp.bfloat16), "rep").astype(jnp.float32),
         lax.psum(part_key.astype(jnp.bfloat16), "rep").astype(jnp.float32),
         lax.psum(part_value.astype(jnp.bfloat16), "rep").astype(jnp.float32),
         lax.psum(part_out.astype(jnp.bfloat16), "rep").astype(jnp.float32),

time: 740 us -> 729 us (0.985)
  blocking collectives: 79.9 us -> 92.5 us
  waiting for transfers between devices: 421 us -> 412 us
  local copies, waits for them, and re-layouts: 73.4 us -> 64.8 us
    reduce_scatter x0 -> x1, waiting for transfers between devices: none -> 29.7 us  [body(): lax.psum_scatter(grad_query_proj.astype(jnp.bfloat16), 'shard', scatter_d...]
    unnamed x19 -> x18, waiting for transfers between devices: 135 us -> 110 us
    all_gather x0 -> x1, blocking collectives: none -> 12.4 us  [summed_here(): shards = lax.all_gather(x, mesh_axis)]
    psum x1, waiting for transfers between devices: 20.3 us -> 8.31 us  [body(): lax.psum(part_key.astype(jnp.bfloat16), 'rep').astype(jnp.float32)]
    unnamed x92 -> x114, local copies, waits for them, and re-layouts: 44.5 us -> 37.5 us
  transfers between devices with their start and end apart: 15 -> 15, of which waited for: 13 -> 13; matrix products, arithmetic and copies ran while one was open for 18% -> 17% of each run, Pallas kernels for 0% -> 0%
where the time goes in v1:
time: 729 us; the launch traced here: 727 us
  waiting for transfers between devices  412 us (57%)
  blocking collectives  92.5 us (13%)
  matrix products  92.1 us (13%)
  local copies, waits for them, and re-layouts  64.8 us (9%)
  other arithmetic  46.6 us (6%)
  between operations  17.3 us (2%)
    unnamed x18, waiting for transfers between devices  110 us
    all_gather x1, waiting for transfers between devices, body(): lax.all_gather(jnp.concatenate([keys, values], axis=1), 'shard', axis=0,...  58 us
    unnamed x2, blocking collectives  56.8 us
    reduce_scatter x1, waiting for transfers between devices, body(): lax.psum_scatter(grad_down.astype(jnp.bfloat16), 'shard', scatter_dimensi...  55.7 us
    reduce_scatter x1, waiting for transfers between devices, body(): lax.psum_scatter(grad_up.astype(jnp.bfloat16), 'shard', scatter_dimension...  55.3 us
    all_gather x1, waiting for transfers between devices, body(): lax.all_gather(w_down, 'shard', axis=0, tiled=True)  46.1 us
    unnamed x114, local copies, waits for them, and re-layouts  37.5 us
    reduce_scatter x1, waiting for transfers between devices, body(): lax.psum_scatter(grad_out_proj.astype(jnp.bfloat16), 'shard', scatter_dim...  31.8 us
  transfers between devices with their start and end apart: 15, of which 13 were waited for; matrix products, arithmetic and copies ran while one was open for 17% of the time, Pallas kernels for 0%

profile of v1, /device:TPU:0, one launch (start us, length us, event | category | flops | bytes accessed | tf_op | source)
XLA Modules:
  0.0 727.1 jit_solution(18072201837707202081)
XLA Ops:
  17.3 30.8 %all-reduce.18 = (bf16[768]{0:T(1024)(128)(2,1)S(1)}, bf16[768]{0:T(1024)(128)(2,1)S(1)}, bf16[768]{0:T(1024)(128)(2,1)S(1)}, bf16[768]{0:T(1024)(128)(2,1)S(1)}...) all-reduce(bf16[768]{0:T(1024)(128)(2,1)S(1)} %dynamic-update-slice, ...), channel_id=1, replica_groups=mesh['rep'=4,'shard'=8] {'shard'}, use_global_device_ids=true, to_apply=%add | all-reduce | flops 5376 | bytes 21504
  50.0 9.5 %all-gather.12.cloned.1.call-done = bf16[768,768]{1,0:T(8,128)(2,1)} async-done(((bf16[96,768]{1,0:T(8,128)(2,1)}), bf16[768,768]{1,0:T(8,128)(2,1)}) %all-gather.12.cloned.1.call-update) | async-done | bytes 1179664 | tf_op jit(solution)/shard_map/all_gather | solution.py:88
  64.8 12.9 %all-gather.1 = bf16[8,1,384]{2,1,0:T(2,128)(2,1)S(1)} all-gather(bf16[1,1,384]{2,1,0:T(2,128)(2,1)S(1)} %reshape.199), channel_id=1, replica_groups=mesh['rep'=4,'shard'=8] {'shard'}, dimensions={0}, use_global_device_ids=true | all-gather | bytes 6912 | tf_op jit(solution)/shard_map/all_gather | solution.py:96
  85.5 58.0 %all-gather.14.cloned.1.call-done = bf16[1792,1536]{1,0:T(8,128)(2,1)} async-done(((bf16[224,1536]{1,0:T(8,128)(2,1)}), bf16[1792,1536]{1,0:T(8,128)(2,1)}) %all-gather.14.cloned.1.call-update) | async-done | bytes 5505040 | tf_op jit(solution)/shard_map/all_gather | solution.py:135
  143.5 8.0 %copy.54 = bf16[1792,1536]{0,1:T(8,128)(2,1)} copy(bf16[1792,1536]{1,0:T(8,128)(2,1)} %all-gather.14.cloned.1.call-done) | data formatting | bytes 11010048
  151.6 25.5 %while.46 = (s32[]{:T(128)}, f32[12,224]{1,0:T(8,128)S(1)}, f32[12,224]{1,0:T(8,128)S(1)}, s32[]{:T(128)}, bf16[1792,1536]{0,1:T(8,128)(2,1)}, /*index=5*/bf16[2...) while((s32[]{:T(128)}, f32[12,224]{1,0:T(8,128)S(1)}, ...), condition=%wide.region_3.4_spmd.clone, body=%wide.region_0.3_spmd.clone.sunk | while | flops 93599368 | bytes 7169450 | solution.py:162
  177.1 34.2 %while.47 = (s32[]{:T(128)}, f32[224,12,64]{0,2,1:T(8,128)}, bf16[1792,1536]{0,1:T(8,128)(2,1)}, s32[]{:T(128)}, bf16[224,12,64]{0,2,1:T(8,128)(2,1)S(1)}, /*ind...) while((s32[]{:T(128)}, f32[224,12,64]{0,2,1:T(8,128)}, ...), condition=%wide.region_5.6_spmd.clone, body=%wide.region_4.5_spmd.clone.sunk | while | flops 179257856 | bytes 4091073 | solution.py:176
  218.9 5.6 multiply_convert_fusion.1
  224.5 46.1 %all-gather.22.cloned.1.call-done = bf16[3072,768]{1,0:T(8,128)(2,1)} async-done(((bf16[384,768]{1,0:T(8,128)(2,1)}), bf16[3072,768]{1,0:T(8,128)(2,1)}) %all-gather.22.cloned.1.call-update) | async-done | bytes 4718608 | tf_op jit(solution)/shard_map/all_gather | solution.py:97
  286.8 44.6 %while.48 = (s32[]{:T(128)}, f32[224,12,64]{0,2,1:T(8,128)S(1)}, bf16[1792,1536]{0,1:T(8,128)(2,1)}, bf16[1792,1536]{0,1:T(8,128)(2,1)}, s32[]{:T(128)}, /*index...) while((s32[]{:T(128)}, f32[224,12,64]{0,2,1:T(8,128)S(1)}, ...), condition=%wide.region_15.16_spmd.clone, body=%wide.region_14.15_spmd.clone.sunk | while | flops 449765888 | bytes 21660152 | solution.py:259
  331.4 8.3 %copy.68 = bf16[1792,1536]{1,0:T(8,128)(2,1)} copy(bf16[1792,1536]{0,1:T(8,128)(2,1)} %get-tuple-element.395) | data formatting | bytes 11010048
  339.7 61.2 %reduce-scatter.22.cloned.1.call-done = bf16[224,1536]{1,0:T(8,128)(2,1)} async-done(((bf16[1792,1536]{1,0:T(8,128)(2,1)}), bf16[224,1536]{1,0:T(8,128)(2,1)}) %reduce-scatter.22.cloned.1.call-update) | async-done | bytes 688144
  408.7 5.0 convolution_convert_fusion.1
  414.8 4.9 convolution_convert_fusion
  422.0 13.4 %reduce-scatter.26.cloned.1.call-done = bf16[96,768]{1,0:T(8,128)(2,1)} async-done(((bf16[768,768]{1,0:T(8,128)(2,1)}), bf16[96,768]{1,0:T(8,128)(2,1)}) %reduce-scatter.26.cloned.1.call-update) | async-done | bytes 147472
  437.2 31.6 %reduce-scatter.28.cloned.1.call-done = bf16[96,768]{1,0:T(8,128)(2,1)} async-done(((bf16[768,768]{1,0:T(8,128)(2,1)}), bf16[96,768]{1,0:T(8,128)(2,1)}) %reduce-scatter.28.cloned.1.call-update) | async-done | bytes 147472
  470.5 31.8 %reduce-scatter.16.cloned.1.call-done = bf16[96,768]{1,0:T(8,128)(2,1)} async-done(((bf16[768,768]{1,0:T(8,128)(2,1)}), bf16[96,768]{1,0:T(8,128)(2,1)}) %reduce-scatter.16.cloned.1.call-update) | async-done | bytes 147472 | tf_op jit(solution)/shard_map/reduce_scatter | solution.py:298
  502.3 55.3 %reduce-scatter.18.cloned.1.call-done = bf16[96,3072]{1,0:T(8,128)(2,1)} async-done(((bf16[768,3072]{1,0:T(8,128)(2,1)}), bf16[96,3072]{1,0:T(8,128)(2,1)}) %reduce-scatter.18.cloned.1.call-update) | async-done | bytes 589840 | tf_op jit(solution)/shard_map/reduce_scatter | solution.py:316
  557.6 55.7 %reduce-scatter.20.cloned.1.call-done = bf16[384,768]{1,0:T(8,128)(2,1)} async-done(((bf16[3072,768]{1,0:T(8,128)(2,1)}), bf16[384,768]{1,0:T(8,128)(2,1)}) %reduce-scatter.20.cloned.1.call-update) | async-done | bytes 589840 | tf_op jit(solution)/shard_map/reduce_scatter | solution.py:322
  617.8 29.7 %reduce-scatter.24.cloned.1.call-done = bf16[96,768]{1,0:T(8,128)(2,1)} async-done(((bf16[768,768]{1,0:T(8,128)(2,1)}), bf16[96,768]{1,0:T(8,128)(2,1)}) %reduce-scatter.24.cloned.1.call-update) | async-done | bytes 147472 | tf_op jit(solution)/shard_map/reduce_scatter | solution.py:289
  647.5 12.4 %all-gather = bf16[384,768]{1,0:T(8,128)(2,1)S(1)} all-gather(bf16[96,768]{1,0:T(8,128)(2,1)} %reduce-scatter.24.cloned.1.call-done), channel_id=2, replica_groups=mesh['rep'=4,'shard'=8] {'rep'}, dimensions={0}, use_global_device_ids=true | all-gather | bytes 737280 | tf_op jit(solution)/shard_map/all_gather | solution.py:14
  660.8 26.0 %all-reduce.17 = (bf16[768]{0:T(1024)(128)(2,1)S(1)}, bf16[768]{0:T(1024)(128)(2,1)S(1)}, bf16[768]{0:T(1024)(128)(2,1)S(1)}, bf16[768]{0:T(1024)(128)(2,1)S(1)}...) all-reduce(bf16[768]{0:T(1024)(128)(2,1)S(1)} %dynamic-update-slice, ...), channel_id=1, replica_groups=mesh['rep'=4,'shard'=8] {'shard'}, use_global_device_ids=true, to_apply=%add.7 | all-reduce | flops 9984 | bytes 39936
  687.5 10.4 %all-reduce.19 = (bf16[96]{0:T(256)(128)(2,1)S(1)}, bf16[96]{0:T(256)(128)(2,1)S(1)}, bf16[96]{0:T(256)(128)(2,1)S(1)}, bf16[96]{0:T(256)(128)(2,1)S(1)}, bf16[9...) all-reduce(bf16[96]{0:T(256)(128)(2,1)S(1)} %dynamic-slice.9, ...), channel_id=1, replica_groups=mesh['rep'=4,'shard'=8] {'rep'}, use_global_device_ids=true, to_apply=%region_27.28 | all-reduce | flops 1152 | bytes 4608 | tf_op jit(solution)/shard_map/psum | solution.py:357
  705.5 8.3 %all-reduce.23.cloned.1.call-done = (bf16[96,768]{0,1:T(8,128)(2,1)}, bf16[96,768]{0,1:T(8,128)(2,1)}, bf16[96,768]{1,0:T(8,128)(2,1)}, bf16[96,3072]{1,0:T(8,128)(2,1)}, bf16[384,768]{1,0:T(8,128)(2,1)}) async-done(((bf16[96,768]{0,1:T(8,128)(2,1)}, bf16[96,768]{0,1:T(8,128)(2,1)}, bf16[96,768]{1,0:T(8,128)(2,1)}, bf16[96,3072]{1,0:T(8,128)(2,1)}, bf16[384,768]{1,0:T(8,128)(2,1)}), ...) | async-done | bytes 1622032 | tf_op jit(solution)/shard_map/psum | solution.py:354
  (354 shorter events, 183.9 us)
Async XLA Ops:
  7.2 41.0 %all-gather.10.cloned.1.call-start = ((), (), s32[]{:S(2)}) async-start(), calls=%async_computation.7 | async-start | bytes 1327104 | tf_op jit(solution)/shard_map/all_gather | solution.py:87
  7.9 51.5 %all-gather.12.cloned.1.call-start = ((), (), s32[]{:S(2)}) async-start(), calls=%async_computation.8 | async-start | bytes 1327104 | tf_op jit(solution)/shard_map/all_gather | solution.py:88
  8.7 74.9 %all-gather.16.cloned.1.call-start = ((), (), s32[]{:S(2)}) async-start(), calls=%async_computation.10 | async-start | bytes 1327104 | tf_op jit(solution)/shard_map/all_gather | solution.py:86
  9.4 134.1 %all-gather.14.cloned.1.call-start = ((), (), s32[]{:S(2)}) async-start(), calls=%async_computation.9 | async-start | bytes 6193152 | tf_op jit(solution)/shard_map/all_gather | solution.py:135
  62.2 150.3 %all-gather.18.cloned.1.call-start = ((), (), s32[]{:S(2)}) async-start(), calls=%async_computation.11 | async-start | bytes 1327104 | tf_op jit(solution)/shard_map/all_gather | solution.py:89
  62.8 156.2 %all-gather.20.cloned.1.call-start = ((), (), s32[]{:S(2)}) async-start(), calls=%async_computation.12 | async-start | bytes 5308416 | tf_op jit(solution)/shard_map/all_gather | solution.py:95
  63.4 207.2 %all-gather.22.cloned.1.call-start = ((), (), s32[]{:S(2)}) async-start(), calls=%async_computation.13 | async-start | bytes 5308416 | tf_op jit(solution)/shard_map/all_gather | solution.py:97
  64.1 336.8 %reduce-scatter.22.cloned.1.call-start = ((), (), s32[]{:S(2)}) async-start(), calls=%async_computation.17 | async-start | bytes 6193152
  214.5 67.0 %copy-start.1 = (f32[224,768]{1,0:T(8,128)}, f32[224,768]{1,0:T(8,128)S(1)}, u32[]{:S(2)}) copy-start(f32[224,768]{1,0:T(8,128)S(1)} %get-tuple-element.678) | copy-start | bytes 2064388
  218.9 51.6 %copy-start.30 = (f32[768]{0:T(1024)S(1)}, f32[768]{0:T(1024)}, u32[]{:S(2)}) copy-start(f32[768]{0:T(1024)} %convert_element_type.255) | copy-start | bytes 9220
  224.5 49.9 %copy-start.13 = (bf16[224,3072]{1,0:T(8,128)(2,1)}, bf16[224,3072]{1,0:T(8,128)(2,1)S(1)}, u32[]{:S(2)}) copy-start(bf16[224,3072]{1,0:T(8,128)(2,1)S(1)} %get-tuple-element.679) | copy-start | bytes 4128772
  339.7 95.8 %reduce-scatter.26.cloned.1.call-start = ((), (), s32[]{:S(2)}) async-start(), calls=%async_computation.19 | async-start | bytes 1327104
  403.9 64.9 %reduce-scatter.28.cloned.1.call-start = ((), (), s32[]{:S(2)}) async-start(), calls=%async_computation.20 | async-start | bytes 1327104
  407.1 95.2 %reduce-scatter.16.cloned.1.call-start = ((), (), s32[]{:S(2)}) async-start(), calls=%async_computation.14 | async-start | bytes 1327104 | tf_op jit(solution)/shard_map/reduce_scatter | solution.py:298
  408.6 149.0 %reduce-scatter.18.cloned.1.call-start = ((), (), s32[]{:S(2)}) async-start(), calls=%async_computation.15 | async-start | bytes 5308416 | tf_op jit(solution)/shard_map/reduce_scatter | solution.py:316
  413.7 199.6 %reduce-scatter.20.cloned.1.call-start = ((), (), s32[]{:S(2)}) async-start(), calls=%async_computation.16 | async-start | bytes 5308416 | tf_op jit(solution)/shard_map/reduce_scatter | solution.py:322
  419.8 227.7 %reduce-scatter.24.cloned.1.call-start = ((), (), s32[]{:S(2)}) async-start(), calls=%async_computation.18 | async-start | bytes 1327104 | tf_op jit(solution)/shard_map/reduce_scatter | solution.py:289
  420.5 194.3 %copy-start.34 = (bf16[96]{0:T(256)(128)(2,1)S(1)}, bf16[96]{0:T(256)(128)(2,1)}, u32[]{:S(2)}) copy-start(bf16[96]{0:T(256)(128)(2,1)} %param.41) | copy-start | bytes 580
  422.0 291.8 %all-reduce.23.cloned.1.call-start = ((), (), s32[]{:S(2)}) async-start(), calls=%async_computation.21 | async-start | bytes 3440640 | tf_op jit(solution)/shard_map/psum | solution.py:354
  613.3 47.4 %copy-start.29 = (bf16[3072]{0:T(1024)(128)(2,1)S(1)}, bf16[3072]{0:T(1024)(128)(2,1)}, u32[]{:S(2)}) copy-start(bf16[3072]{0:T(1024)(128)(2,1)} %get-tuple-element.684) | copy-start | bytes 18436
  613.4 47.4 %copy-start.31 = (bf16[768]{0:T(1024)(128)(2,1)S(1)}, bf16[768]{0:T(1024)(128)(2,1)}, u32[]{:S(2)}) copy-start(bf16[768]{0:T(1024)(128)(2,1)} %get-tuple-element.582) | copy-start | bytes 4612
  613.4 47.4 %copy-start.32 = (bf16[768]{0:T(1024)(128)(2,1)S(1)}, bf16[768]{0:T(1024)(128)(2,1)}, u32[]{:S(2)}) copy-start(bf16[768]{0:T(1024)(128)(2,1)} %get-tuple-element.587) | copy-start | bytes 4612
  613.4 89.2 %copy-start.8 = (bf16[768,768]{1,0:T(8,128)(2,1)S(1)}, bf16[768,768]{1,0:T(8,128)(2,1)}, u32[]{:S(2)}) copy-start(bf16[768,768]{1,0:T(8,128)(2,1)} %all-gather.10.cloned.1.call-done) | copy-start | bytes 3538948
  617.8 84.8 %copy-start.15 = (f32[224,768]{1,0:T(8,128)S(1)}, f32[224,768]{1,0:T(8,128)}, u32[]{:S(2)}) copy-start(f32[224,768]{1,0:T(8,128)} %convolution_add_fusion.3) | copy-start | bytes 2064388
  (37 other events, 243.5 us)
Sparse Core Ops, SparseCore 0:
  9.6 25.6 all-gather.9
  36.9 22.4 all-gather.11
  61.1 22.4 all-gather.15
  85.7 57.7 all-gather.13
  145.0 21.5 all-gather.17
  168.1 50.8 all-gather.19
  220.6 49.9 all-gather.21
  339.8 61.0 reduce-scatter.21
  404.0 31.3 reduce-scatter.25
  437.6 31.1 reduce-scatter.27
  471.1 31.1 reduce-scatter.15
  504.5 53.1 reduce-scatter.17
  559.9 53.3 reduce-scatter.19
  616.0 31.4 reduce-scatter.23
  651.6 62.0 all-reduce.22
